TPU v7x, 128 devices: a whole 4x4x4 slice. The times are simulated.
128 devices in a mesh: seq: 32 (over x, z, core), head: 4 (over y).
Axes of the slice: x: 4, y: 4, z: 4, core: 2. Of those that a mesh axis runs over, the one named last changes fastest.
Arguments:
- inputs: bfloat16 [32768, 6144], P('seq'), may hold values from -6 to 6
- query_vectors: bfloat16 [32768, 4096], P('seq', 'head')
- key_vectors: bfloat16 [32768, 4096], P('seq', 'head'), may hold values from -6 to 6
- value_weight: bfloat16 [6144, 4096], P('seq', 'head'), may hold values from -0.078125 to 0.078125
- log_decay: float32 [32, 32768], P('head', 'seq'), may hold values from -0.8 to 0
- doc_start: int32 [128], P('seq'), may hold values 0 or 1
- norm_gain: float32 [4096], P('head'), may hold values from 0.1 to 1.9
Outputs:
- attended: bfloat16 [32768, 4096], P('seq', 'head')
All inputs are finite; a program needn't handle non-finite values. No bound on the sum of `doc_start` on one device may be relied on, other than what follows from the above.
Results may differ from a plain program's by a relative error of at most 0.0053.
Values may be sent and summed in bfloat16 or wider, within the bound.
No kernel may reach another device: no remote copies, remote signals or barrier semaphores. Data moves between devices by JAX's collectives and lax.ppermute only.
A program may use at most 128 MiB of HBM per device.

v0:
```python
import jax
import jax.numpy as jnp
from jax import lax
from jax.sharding import PartitionSpec as P

SHARD_ATTN_PARTS = 32
E = 128
SPAN = 256


def per_device(inputs, query_vectors, key_vectors, value_weight, log_decay, doc_start, norm_gain):
    tok_rows = inputs.shape[0]
    width_out = value_weight.shape[1]
    head_count = width_out // E
    blocks = tok_rows // SPAN
    values = jnp.dot(
        inputs,
        lax.all_gather(value_weight, "seq", axis=0, tiled=True),
        preferred_element_type=jnp.float32,
    ).astype(jnp.bfloat16)
    query_blocks = query_vectors.reshape(blocks, SPAN, head_count, E)
    key_blocks = key_vectors.reshape(blocks, SPAN, head_count, E)
    value_blocks = values.reshape(blocks, SPAN, head_count, E)
    cumulative = jnp.cumsum(log_decay.reshape(head_count, blocks, SPAN), axis=2)
    cum_blocks = jnp.transpose(cumulative, (1, 0, 2))
    causal = lax.broadcasted_iota(jnp.int32, (SPAN, SPAN), 0) >= lax.broadcasted_iota(
        jnp.int32, (SPAN, SPAN), 1
    )
    scores = jnp.einsum(
        "cihe,cjhe->chij", query_blocks, key_blocks, preferred_element_type=jnp.float32
    )
    gaps = cum_blocks[:, :, :, None] - cum_blocks[:, :, None, :]
    weights = (scores * jnp.exp(jnp.where(causal[None, None], gaps, -1e30))).astype(jnp.bfloat16)
    inner = jnp.einsum("chij,cjhe->cihe", weights, value_blocks, preferred_element_type=jnp.float32)
    span_end = cumulative[:, :, -1]
    key_scale = jnp.transpose(jnp.exp(span_end[:, :, None] - cumulative), (1, 2, 0))[:, :, :, None]
    key_decayed = (key_blocks * key_scale).astype(jnp.bfloat16)
    updates = jnp.einsum(
        "cjhe,cjhf->chef", key_decayed, value_blocks, preferred_element_type=jnp.float32
    )
    survive = 1.0 - doc_start.astype(jnp.float32)
    local_memory = jnp.zeros((head_count, E, E), jnp.float32)
    carry_factor = jnp.ones((head_count,), jnp.float32)
    start_states = []
    start_factors = []
    for block in range(blocks):
        local_memory = local_memory * survive[block]
        carry_factor = carry_factor * survive[block]
        start_states.append(local_memory)
        start_factors.append(carry_factor)
        block_decay = jnp.exp(span_end[:, block])
        local_memory = block_decay[:, None, None] * local_memory + updates[block]
        carry_factor = carry_factor * block_decay
    all_factors, all_states = (
        lax.all_gather(carry_factor[None], "seq", axis=0, tiled=True),
        lax.all_gather(local_memory[None], "seq", axis=0, tiled=True),
    )
    position_now = lax.axis_index("seq")
    ranks = jnp.arange(all_factors.shape[0])
    earlier = (ranks < position_now)[:, None]
    factors_used = jnp.where(earlier, all_factors, 1.0)
    suffix = jnp.cumprod(factors_used[::-1], axis=0)[::-1]
    after = jnp.concatenate([suffix[1:], jnp.ones((1, head_count), jnp.float32)], axis=0)
    weights_sum = jnp.where(earlier, after, 0.0)
    incoming = jnp.einsum("nh,nhef->hef", weights_sum, all_states, precision=lax.Precision.HIGHEST)
    block_states = jnp.stack(start_factors)[:, :, None, None] * incoming[None] + jnp.stack(
        start_states
    )
    query_scale = jnp.transpose(jnp.exp(cumulative), (1, 2, 0))[:, :, :, None]
    query_decayed = query_blocks.astype(jnp.float32) * query_scale
    outer = jnp.einsum(
        "cihe,chef->cihf", query_decayed, block_states, precision=lax.Precision.HIGHEST
    )
    combined = (inner + outer).reshape(tok_rows, width_out)
    local_squares = jnp.sum(combined * combined, axis=1)
    square_total = lax.psum(local_squares, "head")
    mean_square = square_total / (SHARD_ATTN_PARTS * E)
    return (combined * lax.rsqrt(mean_square + 1e-06)[:, None] * norm_gain[None, :]).astype(
        jnp.bfloat16
    )


def solution(mesh):
    placed = (
        P("seq", None),
        P("seq", "head"),
        P("seq", "head"),
        P("seq", "head"),
        P("head", "seq"),
        P("seq"),
        P("head"),
    )
    return jax.shard_map(
        per_device, mesh=mesh, in_specs=placed, out_specs=P("seq", "head"), check_vma=False
    )
```

profile of v0, /device:TPU:0, one launch (start us, length us, event | category | flops | bytes accessed | tf_op | source)
XLA Modules:
  0.0 226.2 jit_solution(371942434578229823)
XLA Ops:
  6.5 0.0 all-gather.4.cloned.1.call-start
  6.5 0.7 all-gather.4.cloned.1.call-update
  7.3 0.0 all-gather.6.cloned.1.call-start
  7.3 0.8 copy.41
  8.1 2.3 reduce-window.6
  10.3 0.2 slice_reduce_fusion
  10.5 0.7 convert_subtract_fusion
  11.2 0.6 fusion.50
  12.5 3.5 %copy.56 = bf16[128,8,8,128]{3,2,1,0:T(8,128)(2,1)} copy(bf16[128,8,8,128]{3,1,2,0:T(8,128)(2,1)} %bitcast.91) | data formatting | bytes 4194304
  16.0 3.0 %copy.44 = bf16[4,256,8,128]{1,3,2,0:T(8,128)(2,1)S(1)} copy(bf16[4,256,8,128]{3,2,1,0:T(8,128)(2,1)} %bitcast.89) | data formatting | bytes 4194304 | tf_op jit(solution)/shard_map/reshape | solution.py:22
  19.0 0.1 copy_bitcast_fusion
  19.1 0.2 slice_reduce_fusion.1
  19.3 0.1 exponential_bitcast_fusion
  19.4 55.7 %all-gather.4.cloned.1.call-done = bf16[6144,1024]{1,0:T(8,128)(2,1)} async-done(((bf16[192,1024]{1,0:T(8,128)(2,1)}), bf16[6144,1024]{1,0:T(8,128)(2,1)}) %all-gather.4.cloned.1.call-update) | async-done | bytes 12582928 | tf_op jit(solution)/shard_map/all_gather | solution.py:18
  75.1 17.4 %convert_bitcast_fusion = bf16[128,8,8,128]{3,1,2,0:T(8,128)(2,1)S(1)} fusion(bf16[1024,6144]{1,0:T(8,128)(2,1)} %param.7, bf16[6144,1024]{1,0:T(8,128)(2,1)} %all-gather.4.cloned.1.call-done), kind=kOutput, calls=%fused_computation.28 | convolution fusion | flops 12885950464 | bytes 27262976 | tf_op jit(solution)/shard_map/dot_general | solution.py:16
  92.5 0.6 copy.54
  93.1 0.0 copy-start
  93.1 0.8 fusion.16
  93.9 0.6 copy-done
  94.4 3.0 %slice_add_fusion = (f32[1,8,128,128]{3,2,1,0:T(8,128)}, f32[1,8,128,128]{3,2,1,0:T(8,128)S(1)}, f32[1,8,128,128]{3,2,1,0:T(8,128)S(1)}, f32[1,8,128,128]{3,2,1,0:T(8,128)}) fusion(f32[4,8,128,128]{3,2,1,0:T(8,128)S(1)} %fusion.16, f32[8]{0:T(128)S(1)} %get-tuple-element.18, f32[]{:T(128)} %bitcast.8, f32[8]{0:T(128)S(1)} %get-tuple-element.19, f32[]{:T(128)} %bitcast.6, ...), kind=kLoop, calls=%fused_computation.36 | loop fusion | flops 1310720 | bytes 4194444 | tf_op jit(solution)/shard_map/add | solution.py:52
  97.4 0.0 all-gather.6.cloned.1.call-update
  97.5 2.6 %fusion.36 = (f32[1,1,8]{2,1,0:T(1,128)S(1)}, f32[1,8]{1,0:T(1,128)S(1)}, f32[1,8]{1,0:T(1,128)S(1)}, f32[1,8]{1,0:T(1,128)S(1)}) fusion(f32[8,4]{0,1:T(4,128)S(1)} %slice_reduce_fusion.1, f32[]{:T(128)} %bitcast.8, f32[]{:T(128)} %bitcast.6, f32[]{:T(128)} %bitcast.3, f32[]{:T(128)} %bitcast.2), kind=kLoop, calls=%fused_computation.55 | loop fusion | flops 56 | bytes 272
  100.0 21.0 %all-gather = f32[32,1,8]{2,1,0:T(1,128)S(1)} all-gather(f32[1,1,8]{2,1,0:T(1,128)S(1)} %get-tuple-element.9), channel_id=1, replica_groups=mesh['seq'=32,'head'=4] {'seq'}, dimensions={0}, use_global_device_ids=true | all-gather | bytes 1056 | tf_op jit(solution)/shard_map/all_gather | solution.py:55
  121.0 0.1 broadcast_select_fusion
  121.1 0.1 reduce_window.9
  121.2 0.1 select_bitcast_fusion
  121.2 0.1 copy.49
  121.3 0.7 pad.5.clone
  122.0 3.6 %copy.55 = bf16[128,8,8,128]{3,2,1,0:T(8,128)(2,1)} copy(bf16[128,8,8,128]{3,1,2,0:T(8,128)(2,1)} %bitcast.92) | data formatting | bytes 4194304
  125.6 0.1 pad_maximum_fusion
  125.7 6.5 %fusion.2 = f32[4,8,128,256]{3,2,1,0:T(8,128)} fusion(f32[4,8,256]{2,1,0:T(8,128)S(1)} %get-tuple-element.16, pred[256,256]{1,0:T(8,128)(4,1)S(1)} %iota_compare_fusion, bf16[4,256,8,128]{1,3,2,0:T(8,128)(2,1)S(1)} %copy.44, bf16[4,256,8,128]{3,2,1,0:T(8,128)(2,1)} %bitcast.86, bf16[4,256,8,128]{3,2,1,0:T(8,128)(2,1)} %bitcast.87), kind=kOutput, calls=%fused_computation.3 | convolution fusion | flops 1082130432 | bytes 10584064 | tf_op jit(solution)/shard_map/chij,cjhe->cihe/dot_general | solution.py:34
  132.2 0.0 copy-start.1
  132.2 37.6 %all-gather.6.cloned.1.call-done = f32[32,8,128,128]{3,2,1,0:T(8,128)} async-done(((f32[1,8,128,128]{3,2,1,0:T(8,128)}), f32[32,8,128,128]{3,2,1,0:T(8,128)}) %all-gather.6.cloned.1.call-update) | async-done | bytes 16777232 | tf_op jit(solution)/shard_map/all_gather | solution.py:56
  169.8 0.0 copy-start.2
  169.8 0.0 copy-start.3
  169.8 22.0 %fusion = f32[8,1,128,128]{3,1,2,0:T(1,128)S(1)} fusion(f32[32,8,1,1]{0,2,3,1:T(1,128)S(1)} %copy.49, f32[32,8,128,128]{3,2,1,0:T(8,128)} %all-gather.6.cloned.1.call-done), kind=kOutput, calls=%fused_computation | convolution fusion | flops 50331648 | bytes 17302528 | tf_op jit(solution)/shard_map/nh,nhef->hef/dot_general | solution.py:65
  191.8 0.0 copy-done.1
  191.8 0.0 copy-done.2
  191.8 0.0 copy-done.3
  191.8 7.6 %multiply_reduce_fusion = (f32[4,256]{1,0:T(4,128)S(1)}, f32[4,256,8,128]{1,3,2,0:T(8,128)}) fusion(f32[4,8,128,256]{3,2,1,0:T(8,128)S(1)} %copy-done.2, f32[4,256,8]{1,2,0:T(8,128)S(1)} %get-tuple-element.13, bf16[4,256,8,128]{3,2,1,0:T(8,128)(2,1)S(1)} %bitcast.88, f32[1,8,128,128]{3,2,1,0:T(8,128)S(1)} %get-tuple-element.6, ...), kind=kOutput, calls=%fused_computation.7 | convolution fusion | flops 1618476032 | bytes 12619920 | tf_op jit(solution)/shard_map/cihe,chef->cihf/dot_general | solution.py:71
  199.4 0.0 copy-start.4
  199.4 5.3 %copy.48 = f32[4,256,8,128]{3,2,1,0:T(8,128)} copy(f32[4,256,8,128]{1,3,2,0:T(8,128)} %get-tuple-element.26) | data formatting | bytes 8388608 | tf_op jit(solution)/shard_map/add | solution.py:74
  204.7 10.5 %psum.7 = f32[1024]{0:T(1024)S(1)} all-reduce(f32[1024]{0:T(1024)S(1)} %bitcast.97), channel_id=1, replica_groups=mesh['seq'=32,'head'=4] {'head'}, use_global_device_ids=true, to_apply=%region_4.5 | all-reduce | flops 1024 | bytes 8192 | tf_op jit(solution)/shard_map/psum | solution.py:76
  215.1 0.0 copy-done.4
  215.1 4.3 %fusion.4 = bf16[1024,1024]{1,0:T(8,128)(2,1)} fusion(f32[128,8,8,128]{3,2,1,0:T(8,128)} %bitcast.84, f32[1024]{0:T(1024)S(1)} %copy-done.4, f32[1024]{0:T(1024)S(1)} %add_rsqrt_fusion), kind=kLoop, calls=%fused_computation.6 | loop fusion | flops 3145728 | bytes 6299648 | tf_op jit(solution)/shard_map/convert_element_type | solution.py:78
  (10 shorter events, 0.1 us)
Async XLA Ops:
  6.5 68.5 %all-gather.4.cloned.1.call-start = ((), (), s32[]{:S(2)}) async-start(), calls=%async_computation | async-start | bytes 12976128 | tf_op jit(solution)/shard_map/all_gather | solution.py:18
  7.3 162.5 %all-gather.6.cloned.1.call-start = ((), (), s32[]{:S(2)}) async-start(), calls=%async_computation.1 | async-start | bytes 17301504 | tf_op jit(solution)/shard_map/all_gather | solution.py:56
  93.1 1.3 copy-start
  132.2 59.6 %copy-start.1 = (bf16[128,8,8,128]{3,2,1,0:T(8,128)(2,1)S(1)}, bf16[128,8,8,128]{3,2,1,0:T(8,128)(2,1)}, u32[]{:S(2)}) copy-start(bf16[128,8,8,128]{3,2,1,0:T(8,128)(2,1)} %copy.55) | copy-start | bytes 6291460
  169.8 22.0 %copy-start.2 = (f32[4,8,128,256]{3,2,1,0:T(8,128)S(1)}, f32[4,8,128,256]{3,2,1,0:T(8,128)}, u32[]{:S(2)}) copy-start(f32[4,8,128,256]{3,2,1,0:T(8,128)} %fusion.2) | copy-start | bytes 12582916
  169.8 22.0 %copy-start.3 = (f32[1,8,128,128]{3,2,1,0:T(8,128)S(1)}, f32[1,8,128,128]{3,2,1,0:T(8,128)}, u32[]{:S(2)}) copy-start(f32[1,8,128,128]{3,2,1,0:T(8,128)} %get-tuple-element.8) | copy-start | bytes 1572868
  199.4 15.7 %copy-start.4 = (f32[1024]{0:T(1024)S(1)}, f32[1024]{0:T(1024)}, u32[]{:S(2)}) copy-start(f32[1024]{0:T(1024)} %param.13) | copy-start | bytes 12292
Sparse Core Ops, SparseCore 0:
  9.6 65.4 all-gather.3
  97.6 72.1 all-gather.5
where the time goes:
time: 227 us; the launch traced here: 226 us
  waiting for transfers between devices  94 us (41%)
  matrix products  54.2 us (24%)
  blocking collectives  31.4 us (14%)
  local copies, waits for them, and re-layouts  19 us (8%)
  between operations  14.2 us (6%)
  other arithmetic  13.3 us (6%)
    all_gather x1, waiting for transfers between devices, per_device(): lax.all_gather(value_weight, 'seq', axis=0, tiled=True)  55.7 us
    all_gather x1, waiting for transfers between devices, per_device(): lax.all_gather(local_memory[None], 'seq', axis=0, tiled=True)  37.6 us
    dot_general x1, matrix products, per_device(): jnp.einsum('nh,nhef->hef', weights_sum, all_states, precision=lax.Precisi...  22 us
    all_gather x1, blocking collectives, per_device(): lax.all_gather(carry_factor[None], 'seq', axis=0, tiled=True)  21 us
    dot_general x1, matrix products, per_device(): jnp.dot(inputs, lax.all_gather(value_weight, 'seq', axis=0, tiled=True),...  17.4 us
    psum x1, blocking collectives, per_device(): square_total = lax.psum(local_squares, 'head')  10.5 us
    unnamed x14, local copies, waits for them, and re-layouts  8.29 us
    dot_general x1, matrix products, per_device(): jnp.einsum('cihe,chef->cihf', query_decayed, block_states, precision=lax....  7.58 us
  transfers between devices with their start and end apart: 2, of which 2 were waited for; matrix products, arithmetic and copies ran while one was open for 11% of the time, Pallas kernels for 0%

commit v1 on v0

--- a/solution.py
+++ b/solution.py
@@ -53,7 +53,10 @@
         carry_factor = carry_factor * block_decay
     all_factors, all_states = (
         lax.all_gather(carry_factor[None], "seq", axis=0, tiled=True),
-        lax.all_gather(local_memory[None], "seq", axis=0, tiled=True),
+        jnp.concatenate(
+            lax.all_to_all(jnp.stack([local_memory[None]] * lax.axis_size("seq")), "seq", 0, 0),
+            axis=0,
+        ),
     )
     position_now = lax.axis_index("seq")
     ranks = jnp.arange(all_factors.shape[0])

time: 227 us -> 463 us (2.04)
  blocking collectives: 31.4 us -> 289 us
  waiting for transfers between devices: 94 us -> 56.5 us
  local copies, waits for them, and re-layouts: 19 us -> 26.8 us
  starting transfers between devices: 0.04 us -> 5.54 us
    all_gather x1, blocking collectives: 21 us -> 279 us  [per_device(): lax.all_gather(carry_factor[None], 'seq', axis=0, tiled=True)]
    all_gather x1 -> x0, waiting for transfers between devices: 37.6 us -> none  [per_device(): lax.all_gather(local_memory[None], 'seq', axis=0, tiled=True)]
    another operation x1 -> x2, local copies, waits for them, and re-layouts: 0.01 us -> 7.84 us  [the longest x1 7.84 us: per_device(): jnp.stack([local_memory[None]] * lax.axis_size('seq'))]
    all_to_all x0 -> x1, starting transfers between devices: none -> 5.54 us  [per_device(): lax.all_to_all(jnp.stack([local_memory[None]] * lax.axis_size('seq')), 's...]
  transfers between devices with their start and end apart: 2 -> 2, of which waited for: 2 -> 1; matrix products, arithmetic and copies ran while one was open for 11% -> 5% of each run, Pallas kernels for 0% -> 0%
where the time goes in v1:
time: 463 us; the launch traced here: 459 us
  blocking collectives  289 us (62%)
  waiting for transfers between devices  56.5 us (12%)
  matrix products  54.3 us (12%)
  local copies, waits for them, and re-layouts  26.8 us (6%)
  between operations  14.2 us (3%)
  other arithmetic  13 us (3%)
  starting transfers between devices  5.54 us (1%)
    all_gather x1, blocking collectives, per_device(): lax.all_gather(carry_factor[None], 'seq', axis=0, tiled=True)  279 us
    all_gather x1, waiting for transfers between devices, per_device(): lax.all_gather(value_weight, 'seq', axis=0, tiled=True)  55.8 us
    dot_general x1, matrix products, per_device(): jnp.einsum('nh,nhef->hef', weights_sum, all_states, precision=lax.Precisi...  22 us
    dot_general x1, matrix products, per_device(): jnp.dot(inputs, lax.all_gather(value_weight, 'seq', axis=0, tiled=True),...  17.4 us
    psum x1, blocking collectives, per_device(): square_total = lax.psum(local_squares, 'head')  10.5 us
  transfers between devices with their start and end apart: 2, of which 1 were waited for; matrix products, arithmetic and copies ran while one was open for 5% of the time, Pallas kernels for 0%

profile of v1, /device:TPU:0, one launch (start us, length us, event | category | flops | bytes accessed | tf_op | source)
XLA Modules:
  0.0 459.4 jit_solution(3480467400247969362)
XLA Ops:
  6.5 0.0 all-gather.3.cloned.1.call-start
  6.5 0.7 all-gather.3.cloned.1.call-update
  7.3 0.8 copy.41
  8.0 2.3 reduce-window.6
  10.3 0.2 slice_reduce_fusion
  10.5 0.7 convert_subtract_fusion
  11.1 0.7 fusion.51
  12.4 3.5 copy.56
  15.9 3.0 copy.44
  18.9 0.1 copy_bitcast_fusion
  19.0 0.2 slice_reduce_fusion.1
  19.2 0.1 exponential_bitcast_fusion
  19.3 55.8 %all-gather.3.cloned.1.call-done = bf16[6144,1024]{1,0:T(8,128)(2,1)} async-done(((bf16[192,1024]{1,0:T(8,128)(2,1)}), bf16[6144,1024]{1,0:T(8,128)(2,1)}) %all-gather.3.cloned.1.call-update) | async-done | bytes 12582928 | tf_op jit(solution)/shard_map/all_gather | solution.py:18
  75.1 17.4 %convert_bitcast_fusion = bf16[128,8,8,128]{3,1,2,0:T(8,128)(2,1)S(1)} fusion(bf16[1024,6144]{1,0:T(8,128)(2,1)} %param.7, bf16[6144,1024]{1,0:T(8,128)(2,1)} %all-gather.3.cloned.1.call-done), kind=kOutput, calls=%fused_computation.28 | convolution fusion | flops 12885950464 | bytes 27262976 | tf_op jit(solution)/shard_map/dot_general | solution.py:16
  92.4 0.6 copy.54
  93.1 0.0 copy-start
  93.1 0.8 fusion.16
  93.9 0.5 copy-done
  94.4 2.8 fusion.33
  97.2 7.8 %stack.26 = f32[32,1,8,128,128]{4,3,2,1,0:T(8,128)} broadcast(f32[8,128,128]{2,1,0:T(8,128)S(1)} %get-tuple-element.5), dimensions={2,3,4} | broadcast | bytes 17301504 | tf_op jit(solution)/shard_map/stack | solution.py:57
  105.1 5.5 %all-to-all-start = ((f32[32,1,8,128,128]{4,3,2,1,0:T(8,128)}), f32[32,1,8,128,128]{4,3,2,1,0:T(8,128)}, u32[]{:S(2)}, u32[]{:S(2)}) async-start(f32[32,1,8,128,128]{4,3,2,1,0:T(8,128)} %stack.26), calls=%async_computation | async-start | bytes 33554432 | tf_op jit(solution)/shard_map/all_to_all | solution.py:57
  110.6 2.5 fusion.37
  113.1 278.6 %all-gather = f32[32,1,8]{2,1,0:T(1,128)S(1)} all-gather(f32[1,1,8]{2,1,0:T(1,128)S(1)} %get-tuple-element.9), channel_id=1, replica_groups=mesh['seq'=32,'head'=4] {'seq'}, dimensions={0}, use_global_device_ids=true | all-gather | bytes 1056 | tf_op jit(solution)/shard_map/all_gather | solution.py:55
  391.7 0.1 broadcast_select_fusion
  391.8 0.1 reduce_window.9
  391.9 0.1 select_bitcast_fusion
  391.9 0.1 copy.49
  392.0 0.6 pad.5.clone
  392.6 3.5 copy.55
  396.2 0.1 pad_maximum_fusion
  396.3 6.6 %fusion.2 = f32[4,8,128,256]{3,2,1,0:T(8,128)} fusion(f32[4,8,256]{2,1,0:T(8,128)S(1)} %get-tuple-element.16, pred[256,256]{1,0:T(8,128)(4,1)S(1)} %iota_compare_fusion, bf16[4,256,8,128]{1,3,2,0:T(8,128)(2,1)S(1)} %copy.44, bf16[4,256,8,128]{3,2,1,0:T(8,128)(2,1)} %bitcast.89, bf16[4,256,8,128]{3,2,1,0:T(8,128)(2,1)} %bitcast.90), kind=kOutput, calls=%fused_computation.3 | convolution fusion | flops 1082130432 | bytes 10584064 | tf_op jit(solution)/shard_map/chij,cjhe->cihe/dot_general | solution.py:34
  402.9 0.0 all-to-all-done
  402.9 0.0 copy-start.1
  402.9 0.0 copy-start.2
  402.9 0.0 copy-start.3
  402.9 22.0 %fusion = f32[8,1,128,128]{3,1,2,0:T(1,128)S(1)} fusion(f32[32,8,1,1]{0,2,3,1:T(1,128)S(1)} %copy.49, f32[32,8,128,128]{3,2,1,0:T(8,128)} %bitcast.19), kind=kOutput, calls=%fused_computation | convolution fusion | flops 50331648 | bytes 17302528 | tf_op jit(solution)/shard_map/nh,nhef->hef/dot_general | solution.py:68
  424.9 0.0 copy-done.1
  424.9 0.0 copy-done.2
  424.9 0.0 copy-done.3
  424.9 7.6 %multiply_reduce_fusion = (f32[4,256]{1,0:T(4,128)S(1)}, f32[4,256,8,128]{1,3,2,0:T(8,128)}) fusion(f32[4,8,128,256]{3,2,1,0:T(8,128)S(1)} %copy-done.2, f32[4,256,8]{1,2,0:T(8,128)S(1)} %get-tuple-element.13, bf16[4,256,8,128]{3,2,1,0:T(8,128)(2,1)S(1)} %bitcast.91, f32[1,8,128,128]{3,2,1,0:T(8,128)S(1)} %get-tuple-element.6, ...), kind=kOutput, calls=%fused_computation.7 | convolution fusion | flops 1618476032 | bytes 12619920 | tf_op jit(solution)/shard_map/cihe,chef->cihf/dot_general | solution.py:74
  432.5 0.0 copy-start.4
  432.5 5.3 %copy.48 = f32[4,256,8,128]{3,2,1,0:T(8,128)} copy(f32[4,256,8,128]{1,3,2,0:T(8,128)} %get-tuple-element.26) | data formatting | bytes 8388608 | tf_op jit(solution)/shard_map/add | solution.py:77
  437.8 10.5 %psum.7 = f32[1024]{0:T(1024)S(1)} all-reduce(f32[1024]{0:T(1024)S(1)} %bitcast.100), channel_id=1, replica_groups=mesh['seq'=32,'head'=4] {'head'}, use_global_device_ids=true, to_apply=%region_4.5 | all-reduce | flops 1024 | bytes 8192 | tf_op jit(solution)/shard_map/psum | solution.py:79
  448.2 0.0 copy-done.4
  448.2 4.3 fusion.4
  (10 shorter events, 0.1 us)
Async XLA Ops:
  6.5 68.5 %all-gather.3.cloned.1.call-start = ((), (), s32[]{:S(2)}) async-start(), calls=%async_computation.1 | async-start | bytes 12976128 | tf_op jit(solution)/shard_map/all_gather | solution.py:18
  93.1 1.3 copy-start
  105.1 297.8 %all-to-all-start = ((f32[32,1,8,128,128]{4,3,2,1,0:T(8,128)}), f32[32,1,8,128,128]{4,3,2,1,0:T(8,128)}, u32[]{:S(2)}, u32[]{:S(2)}) async-start(f32[32,1,8,128,128]{4,3,2,1,0:T(8,128)} %stack.26), calls=%async_computation | async-start | bytes 33554432 | tf_op jit(solution)/shard_map/all_to_all | solution.py:57
  402.9 22.0 %copy-start.1 = (bf16[128,8,8,128]{3,2,1,0:T(8,128)(2,1)S(1)}, bf16[128,8,8,128]{3,2,1,0:T(8,128)(2,1)}, u32[]{:S(2)}) copy-start(bf16[128,8,8,128]{3,2,1,0:T(8,128)(2,1)} %copy.55) | copy-start | bytes 6291460
  402.9 22.0 %copy-start.2 = (f32[4,8,128,256]{3,2,1,0:T(8,128)S(1)}, f32[4,8,128,256]{3,2,1,0:T(8,128)}, u32[]{:S(2)}) copy-start(f32[4,8,128,256]{3,2,1,0:T(8,128)} %fusion.2) | copy-start | bytes 12582916
  402.9 22.0 %copy-start.3 = (f32[1,8,128,128]{3,2,1,0:T(8,128)S(1)}, f32[1,8,128,128]{3,2,1,0:T(8,128)}, u32[]{:S(2)}) copy-start(f32[1,8,128,128]{3,2,1,0:T(8,128)} %get-tuple-element.8) | copy-start | bytes 1572868
  432.5 15.7 %copy-start.4 = (f32[1024]{0:T(1024)S(1)}, f32[1024]{0:T(1024)}, u32[]{:S(2)}) copy-start(f32[1024]{0:T(1024)} %param.13) | copy-start | bytes 12292
Sparse Core Ops, SparseCore 0:
  9.6 65.4 all-gather.2
